TPU v7x, 32 devices: a whole 2x2x4 slice. The times are simulated.
32 devices in a mesh: guide: 2 (over core), blk: 16 (over z, y, x).
Axes of the slice: x: 2, y: 2, z: 4, core: 2. Of those that a mesh axis runs over, the one named last changes fastest.
Arguments:
- x_cols: bfloat16 [128, 2048], P(None, 'blk'), may hold values from -3 to 3
- queries: bfloat16 [128, 9216], P('blk'), may hold values from -64 to 64
- new_kv: bfloat16 [128, 576], P('blk'), may hold values from -6 to 6
- cache: bfloat16 [2, 128, 256, 576], P('guide', 'blk'), may hold values from -8 to 8
- lengths: int32 [2, 128], P('guide'), may hold values from 2 to 256, as said below
- perm: int32 [128], replicated, may hold values from 0 to 127, each once
- guide_scale: float32 [128], replicated, may hold values from 1.5 to 7.5
- w_uv: bfloat16 [16, 512, 128], replicated, may hold values from -0.75 to 0.75
- w_out: bfloat16 [2048, 2048], P(None, 'blk'), may hold values from -0.125 to 0.125
- mlp_gain: float32 [2048], replicated, may hold values from 0.5 to 1.5
- w_gate: bfloat16 [2048, 10944], P(None, 'blk'), may hold values from -0.125 to 0.125
- w_up: bfloat16 [2048, 10944], P(None, 'blk'), may hold values from -0.125 to 0.125
- w_down: bfloat16 [10944, 2048], P('blk'), may hold values from -0.0546875 to 0.0546875
- head_gain: float32 [2048], replicated, may hold values from 0.5 to 1.5
- w_head: bfloat16 [2048, 102400], P(None, 'blk'), may hold values from -0.125 to 0.125
Outputs:
- guided: bfloat16 [128, 102400], P('guide', 'blk')
Inputs may be any that keep to these rules, and one draw needn't show every extreme that they name: Positions 0 to lengths[g, r] - 1 of request r's cache in group g are live; each group has a request with 256 live positions. Slot s holds request perm[s]; every request has one slot.
All inputs are finite; a program needn't handle non-finite values.
Results may differ from a plain program's by a relative error of at most 0.018.
Values may be sent and summed in bfloat16 or wider, within the bound.
No kernel may reach another device: no remote copies, remote signals or barrier semaphores. Data moves between devices by JAX's collectives and lax.ppermute only.
A program may use at most 128 MiB of HBM per device.

v0:
```python
import jax
import jax.numpy as jnp
from jax import lax
from jax.sharding import PartitionSpec as P

FF = 10944


def partner(value, axis, apart):
    mask = 2**apart
    pairs = [(source, source ^ mask) for source in range(lax.axis_size(axis))]
    return lax.ppermute(value, axis, pairs)


def rms_round(hidden, gain):
    values = hidden.astype(jnp.float32)
    meansq = jnp.mean(values * values, axis=-1, keepdims=True)
    return (values * lax.rsqrt(meansq + 1e-06) * gain).astype(jnp.bfloat16)


def body(
    x_cols,
    queries,
    new_kv,
    cache,
    lengths,
    perm,
    guide_scale,
    w_uv,
    w_out,
    mlp_gain,
    w_gate,
    w_up,
    w_down,
    head_gain,
    w_head,
):
    guide_index = lax.axis_index("guide")
    blk_index = lax.axis_index("blk")
    slots_dev = queries.shape[0]
    heads_count = w_uv.shape[0]
    latent_size = w_uv.shape[1]
    key_width = new_kv.shape[1]
    score_scale = (w_uv.shape[2] + key_width - latent_size) ** (-0.5)
    slot_ids = blk_index * slots_dev + jnp.arange(slots_dev, dtype=jnp.int32)
    owners = jnp.take(perm, slot_ids)
    live_len = jnp.take(lengths[0], owners)
    query_heads = queries.reshape(slots_dev, heads_count, key_width)
    cached_keys = cache[0]
    scores = (
        jnp.einsum("shk,slk->shl", query_heads, cached_keys, preferred_element_type=jnp.float32)
        * score_scale
    )
    own_score = (
        jnp.einsum("shk,sk->sh", query_heads, new_kv, preferred_element_type=jnp.float32)
        * score_scale
    )
    live_mask = (
        jnp.arange(cached_keys.shape[1], dtype=jnp.int32)[None, None, :] < live_len[:, None, None]
    )
    scores = jnp.where(live_mask, scores, jnp.float32(-1e30))
    peak_score = jnp.maximum(jnp.max(scores, axis=-1), own_score)
    probs = jnp.where(live_mask, jnp.exp(scores - peak_score[..., None]), jnp.float32(0.0))
    own_prob = jnp.exp(own_score - peak_score)
    softmax_total = jnp.sum(probs, axis=-1) + own_prob
    weights = (probs / softmax_total[..., None]).astype(jnp.bfloat16)
    own_weight = (own_prob / softmax_total).astype(jnp.bfloat16)
    latent_out = jnp.einsum(
        "shl,slc->shc", weights, cached_keys[:, :, :latent_size], preferred_element_type=jnp.float32
    )
    latent_out = latent_out + own_weight.astype(jnp.float32)[..., None] * new_kv[
        :, None, :latent_size
    ].astype(jnp.float32)
    value_rows = jnp.einsum(
        "shc,hcd->shd", latent_out.astype(jnp.bfloat16), w_uv, preferred_element_type=jnp.float32
    )
    value_rows = value_rows.astype(jnp.bfloat16).reshape(slots_dev, -1)
    attended = jnp.dot(
        lax.all_gather(value_rows, "blk", axis=0, tiled=True),
        w_out,
        preferred_element_type=jnp.float32,
    )
    residual = (x_cols.astype(jnp.float32) + attended).astype(jnp.bfloat16)
    rows_full = lax.all_gather(residual, "blk", axis=1, tiled=True)
    normed = rms_round(rows_full, mlp_gain)
    unit_count = w_gate.shape[1]
    gate_out = jnp.dot(normed, w_gate, preferred_element_type=jnp.float32)
    up_out = jnp.dot(normed, w_up, preferred_element_type=jnp.float32)
    unit_ids = blk_index * unit_count + jnp.arange(unit_count, dtype=jnp.int32)
    hidden = jnp.where(
        unit_ids[None, :] < FF, jax.nn.silu(gate_out) * up_out, jnp.float32(0.0)
    ).astype(jnp.bfloat16)
    partial_sum = jnp.dot(hidden, w_down, preferred_element_type=jnp.float32)
    summed = lax.psum(partial_sum, "blk")
    after_mlp = (rows_full.astype(jnp.float32) + summed).astype(jnp.bfloat16)
    logits = jnp.dot(rms_round(after_mlp, head_gain), w_head, preferred_element_type=jnp.float32)
    request_count = logits.shape[0]
    half_rows = request_count // 2
    slot_scale = jnp.take(guide_scale, perm)
    request_order = (
        jnp.zeros((request_count,), jnp.int32)
        .at[perm]
        .set(jnp.arange(request_count, dtype=jnp.int32))
    )
    own_order = lax.dynamic_slice_in_dim(request_order, guide_index * half_rows, half_rows)
    other_logits = partner(logits.astype(jnp.bfloat16), "guide", 0).astype(logits.dtype)
    cond_logits = jnp.where(guide_index == 0, logits, other_logits)
    uncond_logits = jnp.where(guide_index == 0, other_logits, logits)
    mixed = (uncond_logits + slot_scale[:, None] * (cond_logits - uncond_logits)).astype(
        jnp.bfloat16
    )
    return jnp.take(mixed, own_order, axis=0)


def solution(mesh):
    return jax.shard_map(
        body,
        mesh=mesh,
        in_specs=(
            P(None, "blk"),
            P("blk", None),
            P("blk", None),
            P("guide", "blk", None, None),
            P("guide", None),
            P(),
            P(),
            P(),
            P(None, "blk"),
            P(),
            P(None, "blk"),
            P(None, "blk"),
            P("blk", None),
            P(),
            P(None, "blk"),
        ),
        out_specs=P("guide", "blk"),
        check_vma=False,
    )
```

profile of v0, /device:TPU:0, one launch (start us, length us, event | category | flops | bytes accessed | tf_op | source)
XLA Modules:
  0.0 257.7 jit_solution(10083849745343940406)
XLA Ops:
  6.5 0.0 copy-start
  6.5 0.0 all-reduce.2.cloned.1.call-start
  6.5 1.2 reshape.73
  7.8 1.3 gather_fusion.2
  9.1 1.3 gather_fusion.3
  10.4 0.1 iota_compare_fusion
  10.5 0.7 slice_convert_fusion
  11.2 0.9 fusion.44
  12.1 2.2 fusion.55
  14.3 0.2 fusion.39
  14.5 0.1 copy.17
  14.6 0.0 copy-start.3
  14.6 0.0 copy-start.4
  14.6 0.0 copy-start.6
  14.6 2.4 fusion.4
  17.0 0.0 copy-done.3
  17.0 0.0 copy-start.7
  17.0 0.5 fusion.11
  17.5 45.3 %all_gather.6 = bf16[128,2048]{1,0:T(8,128)(2,1)S(1)} all-gather(bf16[8,2048]{1,0:T(8,128)(2,1)S(1)} %fusion.11), channel_id=1, replica_groups=mesh['guide'=2,'blk'=16] {'blk'}, dimensions={0}, use_global_device_ids=true | all-gather | bytes 557056 | tf_op jit(solution)/shard_map/all_gather | solution.py:79
  62.8 0.0 copy-done.4
  62.8 0.0 copy-done.6
  62.8 0.3 fusion.10
  63.1 38.5 %all_gather.7 = bf16[128,2048]{1,0:T(8,128)(2,1)S(1)} all-gather(bf16[128,128]{1,0:T(8,128)(2,1)S(1)} %fusion.10), channel_id=1, replica_groups=mesh['guide'=2,'blk'=16] {'blk'}, dimensions={1}, use_global_device_ids=true | all-gather | bytes 557056 | tf_op jit(solution)/shard_map/all_gather | solution.py:84
  101.7 0.2 fusion.15
  101.9 0.0 copy-done.7
  101.9 3.5 %fusion.34 = f32[128,684]{0,1:T(8,128)} fusion(bf16[2048,684]{0,1:T(8,128)(2,1)} %param.27, bf16[128,2048]{1,0:T(8,128)(2,1)S(1)} %all_gather.7, f32[2048]{0:T(1024)S(1)} %copy-done.7, f32[128]{0:T(128)S(1)} %add_rsqrt_fusion.1), kind=kOutput, calls=%fused_computation.49 | convolution fusion | flops 359661568 | bytes 3684864 | tf_op jit(solution)/shard_map/dot_general | solution.py:87
  105.4 0.0 copy-done
  105.4 0.0 copy-start.5
  105.4 5.0 %fusion.8 = f32[128,2048]{1,0:T(8,128)} fusion(bf16[684,2048]{1,0:T(8,128)(2,1)S(1)} %copy-done, bf16[2048,684]{0,1:T(8,128)(2,1)} %param.28, f32[128,684]{0,1:T(8,128)} %fusion.34, pred[684]{0:T(1024)(128)(4,1)S(1)} %add_compare_fusion, bf16[128,2048]{1,0:T(8,128)(2,1)S(1)} %all_gather.7, f32[2048]{0:T(1024)S(1)} %copy-done.7, f32[128]{0:T(128)S(1)} %add_rsqrt_fusion.1), kind=kOutput, calls=%fused_computation.21 | convolution fusion | flops 718887424 | bytes 7535788 | tf_op jit(solution)/shard_map/dot_general | solution.py:93
  110.4 0.0 all-reduce.2.cloned.1.call-update
  110.5 109.6 %all-reduce.2.cloned.1.call-done = f32[128,2048]{1,0:T(8,128)} async-done(((f32[128,2048]{1,0:T(8,128)}), f32[128,2048]{1,0:T(8,128)}) %all-reduce.2.cloned.1.call-update) | async-done | bytes 1048592 | tf_op jit(solution)/shard_map/psum | solution.py:94
  220.1 1.4 fusion.12
  221.5 0.0 copy-done.5
  221.5 0.0 copy-start.2
  221.5 0.0 copy-start.1
  221.5 14.7 %fusion.56 = (bf16[128,6400]{1,0:T(8,128)(2,1)}, f32[128,6400]{1,0:T(8,128)}) fusion(bf16[2048,6400]{1,0:T(8,128)(2,1)} %param.31, f32[2048]{0:T(1024)S(1)} %copy-done.5, f32[128]{0:T(128)S(1)} %add_rsqrt_fusion, f32[128,2048]{1,0:T(8,128)} %all-reduce.2.cloned.1.call-done, bf16[128,2048]{1,0:T(8,128)(2,1)S(1)} %all_gather.7), kind=kOutput, calls=%fused_computation.90 | convolution fusion | flops 3358097408 | bytes 32711168 | tf_op jit(solution)/shard_map/dot_general | solution.py:96
  236.2 0.0 collective-permute-start
  236.2 0.0 copy-done.2
  236.2 1.2 scatter_custom_fusion
  237.4 0.0 copy-done.1
  237.4 1.2 gather_fusion
  238.6 0.1 compare_and_fusion
  238.8 1.3 collective-permute-done
  240.1 4.3 %fusion.3 = bf16[128,6400]{1,0:T(8,128)(2,1)} fusion(f32[128,6400]{1,0:T(8,128)} %get-tuple-element.13, bf16[128,6400]{1,0:T(8,128)(2,1)} %collective-permute-done, f32[128]{0:T(128)S(1)} %and_select_fusion.2, pred[]{:T(512)S(6)} %eq.4), kind=kLoop, calls=%fused_computation.10 | loop fusion | flops 5734400 | bytes 6554113 | tf_op jit(solution)/shard_map/convert_element_type | solution.py:109
  244.4 4.3 %gather_fusion.1 = bf16[64,6400]{1,0:T(8,128)(2,1)} fusion(bf16[128,6400]{1,0:T(8,128)(2,1)} %fusion.3, s32[1024]{0:T(1024)S(1)} %pad_clamp_fusion), kind=kCustom, calls=%fused_computation.3 | custom fusion | bytes 1638656 | tf_op jit(solution)/shard_map/jit(_take)/gather | solution.py:112
  248.7 2.2 broadcast_select_fusion
  (15 shorter events, 0.1 us)
Async XLA Ops:
  6.5 98.9 %copy-start = (bf16[684,2048]{1,0:T(8,128)(2,1)S(1)}, bf16[684,2048]{1,0:T(8,128)(2,1)}, u32[]{:S(2)}) copy-start(bf16[684,2048]{1,0:T(8,128)(2,1)} %param.29) | copy-start | bytes 8404996
  6.5 213.5 %all-reduce.2.cloned.1.call-start = ((), (), s32[]{:S(2)}) async-start(), calls=%async_computation | async-start | bytes 2097152 | tf_op jit(solution)/shard_map/psum | solution.py:94
  14.6 2.4 copy-start.3
  14.6 48.3 %copy-start.4 = (bf16[2048,128]{1,0:T(8,128)(2,1)S(1)}, bf16[2048,128]{1,0:T(8,128)(2,1)}, u32[]{:S(2)}) copy-start(bf16[2048,128]{1,0:T(8,128)(2,1)} %param.25) | copy-start | bytes 1572868
  14.6 48.3 %copy-start.6 = (bf16[128,128]{1,0:T(8,128)(2,1)S(1)}, bf16[128,128]{1,0:T(8,128)(2,1)}, u32[]{:S(2)}) copy-start(bf16[128,128]{1,0:T(8,128)(2,1)} %param.17) | copy-start | bytes 98308
  17.0 84.9 %copy-start.7 = (f32[2048]{0:T(1024)S(1)}, f32[2048]{0:T(1024)}, u32[]{:S(2)}) copy-start(f32[2048]{0:T(1024)} %param.26) | copy-start | bytes 24580
  105.4 116.1 %copy-start.5 = (f32[2048]{0:T(1024)S(1)}, f32[2048]{0:T(1024)}, u32[]{:S(2)}) copy-start(f32[2048]{0:T(1024)} %param.30) | copy-start | bytes 24580
  221.5 14.7 %copy-start.2 = (s32[128]{0:T(128)S(1)}, s32[128]{0:T(128)}, u32[]{:S(2)}) copy-start(s32[128]{0:T(128)} %param.22) | copy-start | bytes 1540
  221.5 15.9 %copy-start.1 = (f32[128]{0:T(128)S(1)}, f32[128]{0:T(128)}, u32[]{:S(2)}) copy-start(f32[128]{0:T(128)} %param.23) | copy-start | bytes 1540
  236.2 3.8 %collective-permute-start = (bf16[128,6400]{1,0:T(8,128)(2,1)}, bf16[128,6400]{1,0:T(8,128)(2,1)}, u32[]{:S(2)}, u32[]{:S(2)}) collective-permute-start(bf16[128,6400]{1,0:T(8,128)(2,1)} %get-tuple-element.12), channel_id=1, source_target_pairs={{0,16},{16,0},{1,17},{17,1},{2,18},{18,2},{3,19},{19,3},{4,20},{20... | collective-permute-start | bytes 4915208 | tf_op jit(solution)/shard_map/ppermute | solution.py:12
Sparse Core Ops, SparseCore 0:
  110.6 109.4 all-reduce.1
where the time goes:
time: 258 us
  waiting for transfers between devices  111 us (43%)
  blocking collectives  83.9 us (33%)
  matrix products  29.5 us (11%)
  between operations  13.5 us (5%)
  local copies, waits for them, and re-layouts  10.7 us (4%)
  other arithmetic  9.26 us (4%)
    psum x1, waiting for transfers between devices, body(): summed = lax.psum(partial_sum, 'blk')  110 us
    all_gather x1, blocking collectives, body(): lax.all_gather(value_rows, 'blk', axis=0, tiled=True)  45.3 us
    all_gather x1, blocking collectives, body(): rows_full = lax.all_gather(residual, 'blk', axis=1, tiled=True)  38.5 us
    dot_general x1, matrix products, body(): jnp.dot(rms_round(after_mlp, head_gain), w_head, preferred_element_type=j...  14.7 us
  transfers between devices with their start and end apart: 2, of which 2 were waited for; matrix products, arithmetic and copies ran while one was open for 1% of the time, Pallas kernels for 0%

commit v1 on v0

--- a/solution.py
+++ b/solution.py
@@ -2,6 +2,7 @@
 import jax.numpy as jnp
 from jax import lax
 from jax.sharding import PartitionSpec as P
+from jax.lax import axis_size, ppermute
 
 FF = 10944
 
@@ -91,7 +92,17 @@
         unit_ids[None, :] < FF, jax.nn.silu(gate_out) * up_out, jnp.float32(0.0)
     ).astype(jnp.bfloat16)
     partial_sum = jnp.dot(hidden, w_down, preferred_element_type=jnp.float32)
-    summed = lax.psum(partial_sum, "blk")
+
+    def sides_mark(mine, comm_axis):
+        nodes = axis_size(comm_axis)
+        w2 = mine
+        for to_i in [
+            [(no, no ^ dev_j) for no in range(nodes)] for dev_j in (1, 2, 4, 8, 16) if dev_j < nodes
+        ]:
+            w2 = w2 + ppermute(w2, comm_axis, to_i)
+        return w2
+
+    summed = sides_mark(partial_sum, "blk")
     after_mlp = (rows_full.astype(jnp.float32) + summed).astype(jnp.bfloat16)
     logits = jnp.dot(rms_round(after_mlp, head_gain), w_head, preferred_element_type=jnp.float32)
     request_count = logits.shape[0]

time: 258 us -> 217 us (0.84)
  waiting for transfers between devices: 111 us -> 80 us
  between operations: 13.5 us -> 0.23 us
    psum x1 -> x0, waiting for transfers between devices: 110 us -> none  [body(): summed = lax.psum(partial_sum, 'blk')]
    ppermute x0 -> x4, waiting for transfers between devices: none -> 78.7 us  [sides_mark(): w2 = w2 + ppermute(w2, comm_axis, to_i)]
  transfers between devices with their start and end apart: 2 -> 5, of which waited for: 2 -> 5; matrix products, arithmetic and copies ran while one was open for 1% -> 1% of each run, Pallas kernels for 0% -> 0%
where the time goes in v1:
time: 217 us; the launch traced here: 216 us
  blocking collectives  84 us (39%)
  waiting for transfers between devices  80 us (37%)
  matrix products  29.1 us (13%)
  local copies, waits for them, and re-layouts  10.7 us (5%)
  other arithmetic  9.78 us (5%)
  starting transfers between devices  2.43 us (1%)
    ppermute x4, waiting for transfers between devices, sides_mark(): w2 = w2 + ppermute(w2, comm_axis, to_i)  78.7 us
    all_gather x1, blocking collectives, body(): lax.all_gather(value_rows, 'blk', axis=0, tiled=True)  45.3 us
    all_gather x1, blocking collectives, body(): rows_full = lax.all_gather(residual, 'blk', axis=1, tiled=True)  38.7 us
    dot_general x1, matrix products, body(): jnp.dot(rms_round(after_mlp, head_gain), w_head, preferred_element_type=j...  14.3 us
    dot_general x1, matrix products, body(): partial_sum = jnp.dot(hidden, w_down, preferred_element_type=jnp.float32)  5.01 us
    convert_element_type x1, other arithmetic, body(): (uncond_logits + slot_scale[:, None] * (cond_logits - uncond_logits)).ast...  4.36 us
    gather x1, local copies, waits for them, and re-layouts, body(): return jnp.take(mixed, own_order, axis=0)  4.35 us
  transfers between devices with their start and end apart: 5, of which 5 were waited for; matrix products, arithmetic and copies ran while one was open for 1% of the time, Pallas kernels for 0%

profile of v1, /device:TPU:0, one launch (start us, length us, event | category | flops | bytes accessed | tf_op | source)
XLA Modules:
  0.0 216.3 jit_solution(16089499453523218442)
XLA Ops:
  0.0 0.0 copy-start
  0.0 1.2 reshape.73
  1.3 1.3 gather_fusion.2
  2.6 1.3 gather_fusion.3
  3.9 0.1 iota_compare_fusion
  4.0 0.7 slice_convert_fusion
  4.7 0.9 fusion.44
  5.5 2.2 %fusion.55 = (f32[8,16]{1,0:T(8,128)S(1)}, f32[8,16,256]{2,1,0:T(8,128)S(1)}) fusion(bf16[8,16,576]{2,1,0:T(8,128)(2,1)S(1)} %reshape.73, bf16[1,8,256,576]{2,3,1,0:T(8,128)(2,1)} %param.20, pred[8,256]{1,0:T(8,128)(4,1)S(1)} %iota_compare_fusion), kind=kOutput, calls=%fused_computation.89 | convolution fusion | flops 37846912 | bytes 2640384 | tf_op jit(solution)/shard_map/shk,slk->shl/dot_general | solution.py:52
  7.7 0.2 fusion.39
  8.0 0.1 copy.17
  8.0 2.4 %fusion.4 = f32[8,16,512]{2,1,0:T(8,128)S(1)} fusion(bf16[8,256,576]{1,2,0:T(8,128)(2,1)} %bitcast.23, f32[8,16,256]{2,1,0:T(8,128)S(1)} %get-tuple-element.13, f32[8,16]{1,0:T(8,128)S(1)} %get-tuple-element.11, f32[8,16]{1,0:T(8,128)S(1)} %multiply_maximum_fusion, pred[8,256]{1,0:T(8,128)(4,1)S(1)} %iota_compare_fusion), kind=kOutput, calls=%fused_computation.11 | convolution fusion | flops 33685504 | bytes 2493440 | tf_op jit(solution)/shard_map/shl,slc->shc/dot_general | solution.py:69
  10.4 0.0 copy-done.3
  10.4 0.5 fusion.11
  11.0 45.3 %all_gather.6 = bf16[128,2048]{1,0:T(8,128)(2,1)S(1)} all-gather(bf16[8,2048]{1,0:T(8,128)(2,1)S(1)} %fusion.11), channel_id=1, replica_groups=mesh['guide'=2,'blk'=16] {'blk'}, dimensions={0}, use_global_device_ids=true | all-gather | bytes 557056 | tf_op jit(solution)/shard_map/all_gather | solution.py:80
  56.3 0.0 copy-done.4
  56.3 0.0 copy-done.6
  56.3 0.3 fusion.10
  56.6 38.7 %all_gather.7 = bf16[128,2048]{1,0:T(8,128)(2,1)S(1)} all-gather(bf16[128,128]{1,0:T(8,128)(2,1)S(1)} %fusion.10), channel_id=1, replica_groups=mesh['guide'=2,'blk'=16] {'blk'}, dimensions={1}, use_global_device_ids=true | all-gather | bytes 557056 | tf_op jit(solution)/shard_map/all_gather | solution.py:85
  95.3 0.2 fusion.15
  95.5 0.0 copy-done.7
  95.5 3.5 %fusion.34 = f32[128,684]{0,1:T(8,128)} fusion(bf16[2048,684]{0,1:T(8,128)(2,1)} %param.27, bf16[128,2048]{1,0:T(8,128)(2,1)S(1)} %all_gather.7, f32[2048]{0:T(1024)S(1)} %copy-done.7, f32[128]{0:T(128)S(1)} %add_rsqrt_fusion.1), kind=kOutput, calls=%fused_computation.49 | convolution fusion | flops 359661568 | bytes 3684864 | tf_op jit(solution)/shard_map/dot_general | solution.py:88
  99.0 5.0 %fusion.8 = f32[128,2048]{1,0:T(8,128)} fusion(bf16[684,2048]{1,0:T(8,128)(2,1)S(1)} %copy-done, bf16[2048,684]{0,1:T(8,128)(2,1)} %param.28, f32[128,684]{0,1:T(8,128)} %fusion.34, pred[684]{0:T(1024)(128)(4,1)S(1)} %add_compare_fusion, bf16[128,2048]{1,0:T(8,128)(2,1)S(1)} %all_gather.7, f32[2048]{0:T(1024)S(1)} %copy-done.7, f32[128]{0:T(128)S(1)} %add_rsqrt_fusion.1), kind=kOutput, calls=%fused_computation.21 | convolution fusion | flops 718887424 | bytes 7535788 | tf_op jit(solution)/shard_map/dot_general | solution.py:94
  104.0 2.2 %collective-permute-start = (f32[128,2048]{1,0:T(8,128)}, f32[128,2048]{1,0:T(8,128)S(1)}, u32[]{:S(2)}, u32[]{:S(2)}) collective-permute-start(f32[128,2048]{1,0:T(8,128)} %fusion.8), channel_id=1, source_target_pairs={{0,1},{1,0},{2,3},{3,2},{4,5},{5,4},{6,7},{7,6},{8,9},{9,8},{10,11... | collective-permute-start | bytes 3145736 | tf_op jit(solution)/shard_map/ppermute | solution.py:102
  106.2 13.0 %collective-permute-done = f32[128,2048]{1,0:T(8,128)S(1)} collective-permute-done((f32[128,2048]{1,0:T(8,128)}, f32[128,2048]{1,0:T(8,128)S(1)}, u32[]{:S(2)}, u32[]{:S(2)}) %collective-permute-start) | collective-permute-done | bytes 1048608 | tf_op jit(solution)/shard_map/ppermute | solution.py:102
  119.2 1.3 add.101
  120.6 0.1 collective-permute-start.1
  120.6 14.8 %collective-permute-done.1 = f32[128,2048]{1,0:T(8,128)S(1)} collective-permute-done((f32[128,2048]{1,0:T(8,128)S(1)}, f32[128,2048]{1,0:T(8,128)S(1)}, u32[]{:S(2)}, u32[]{:S(2)}) %collective-permute-start.1) | collective-permute-done | bytes 1048608 | tf_op jit(solution)/shard_map/ppermute | solution.py:102
  135.4 0.1 add.102
  135.6 0.0 copy-start.5
  135.6 0.1 collective-permute-start.2
  135.6 25.1 %collective-permute-done.2 = f32[128,2048]{1,0:T(8,128)S(1)} collective-permute-done((f32[128,2048]{1,0:T(8,128)S(1)}, f32[128,2048]{1,0:T(8,128)S(1)}, u32[]{:S(2)}, u32[]{:S(2)}) %collective-permute-start.2) | collective-permute-done | bytes 1048608 | tf_op jit(solution)/shard_map/ppermute | solution.py:102
  160.7 0.1 add.103
  160.8 0.1 collective-permute-start.3
  160.9 25.9 %collective-permute-done.3 = f32[128,2048]{1,0:T(8,128)S(1)} collective-permute-done((f32[128,2048]{1,0:T(8,128)S(1)}, f32[128,2048]{1,0:T(8,128)S(1)}, u32[]{:S(2)}, u32[]{:S(2)}) %collective-permute-start.3) | collective-permute-done | bytes 1048608 | tf_op jit(solution)/shard_map/ppermute | solution.py:102
  186.8 0.3 fusion.12
  187.2 0.0 copy-start.2
  187.2 0.0 copy-start.1
  187.2 14.3 %fusion.56 = (bf16[128,6400]{1,0:T(8,128)(2,1)}, f32[128,6400]{1,0:T(8,128)}) fusion(bf16[2048,6400]{1,0:T(8,128)(2,1)} %param.31, bf16[128,2048]{1,0:T(8,128)(2,1)S(1)} %get-tuple-element.9, f32[2048]{0:T(1024)S(1)} %copy-done.5, f32[128]{0:T(128)S(1)} %add_rsqrt_fusion), kind=kOutput, calls=%fused_computation.90 | convolution fusion | flops 3357310976 | bytes 31662592 | tf_op jit(solution)/shard_map/dot_general | solution.py:107
  201.5 0.0 collective-permute-start.4
  201.6 0.0 copy-done.2
  201.6 1.2 scatter_custom_fusion
  202.7 0.0 copy-done.1
  202.8 1.2 gather_fusion
  204.0 0.1 compare_and_fusion
  204.1 1.3 collective-permute-done.4
  205.4 4.4 %fusion.3 = bf16[128,6400]{1,0:T(8,128)(2,1)} fusion(f32[128,6400]{1,0:T(8,128)} %get-tuple-element.15, bf16[128,6400]{1,0:T(8,128)(2,1)} %collective-permute-done.4, f32[128]{0:T(128)S(1)} %and_select_fusion.2, pred[]{:T(512)S(6)} %eq.4), kind=kLoop, calls=%fused_computation.10 | loop fusion | flops 5734400 | bytes 6554113 | tf_op jit(solution)/shard_map/convert_element_type | solution.py:120
  209.8 4.3 %gather_fusion.1 = bf16[64,6400]{1,0:T(8,128)(2,1)} fusion(bf16[128,6400]{1,0:T(8,128)(2,1)} %fusion.3, s32[1024]{0:T(1024)S(1)} %pad_clamp_fusion), kind=kCustom, calls=%fused_computation.3 | custom fusion | bytes 1638656 | tf_op jit(solution)/shard_map/jit(_take)/gather | solution.py:123
  214.1 2.2 %broadcast_select_fusion = bf16[64,6400]{1,0:T(8,128)(2,1)} fusion(bf16[64,6400]{1,0:T(8,128)(2,1)} %gather_fusion.1, pred[64]{0:T(512)(128)(4,1)S(1)} %get-tuple-element.6), kind=kLoop, calls=%fused_computation.35 | loop fusion | flops 409600 | bytes 1638464 | tf_op jit(solution)/shard_map/jit(_take)/select_n | solution.py:123
  (21 shorter events, 0.1 us)
Async XLA Ops:
  0.0 99.0 %copy-start = (bf16[684,2048]{1,0:T(8,128)(2,1)S(1)}, bf16[684,2048]{1,0:T(8,128)(2,1)}, u32[]{:S(2)}) copy-start(bf16[684,2048]{1,0:T(8,128)(2,1)} %param.29) | copy-start | bytes 8404996
  8.0 2.4 %copy-start.3 = (bf16[16,512,128]{2,1,0:T(8,128)(2,1)S(1)}, bf16[16,512,128]{2,1,0:T(8,128)(2,1)}, u32[]{:S(2)}) copy-start(bf16[16,512,128]{2,1,0:T(8,128)(2,1)} %param.24) | copy-start | bytes 6291460
  8.0 48.3 %copy-start.4 = (bf16[2048,128]{1,0:T(8,128)(2,1)S(1)}, bf16[2048,128]{1,0:T(8,128)(2,1)}, u32[]{:S(2)}) copy-start(bf16[2048,128]{1,0:T(8,128)(2,1)} %param.25) | copy-start | bytes 1572868
  8.0 48.3 %copy-start.6 = (bf16[128,128]{1,0:T(8,128)(2,1)S(1)}, bf16[128,128]{1,0:T(8,128)(2,1)}, u32[]{:S(2)}) copy-start(bf16[128,128]{1,0:T(8,128)(2,1)} %param.17) | copy-start | bytes 98308
  10.4 85.1 %copy-start.7 = (f32[2048]{0:T(1024)S(1)}, f32[2048]{0:T(1024)}, u32[]{:S(2)}) copy-start(f32[2048]{0:T(1024)} %param.26) | copy-start | bytes 24580
  104.0 15.2 %collective-permute-start = (f32[128,2048]{1,0:T(8,128)}, f32[128,2048]{1,0:T(8,128)S(1)}, u32[]{:S(2)}, u32[]{:S(2)}) collective-permute-start(f32[128,2048]{1,0:T(8,128)} %fusion.8), channel_id=1, source_target_pairs={{0,1},{1,0},{2,3},{3,2},{4,5},{5,4},{6,7},{7,6},{8,9},{9,8},{10,11... | collective-permute-start | bytes 3145736 | tf_op jit(solution)/shard_map/ppermute | solution.py:102
  120.6 14.9 %collective-permute-start.1 = (f32[128,2048]{1,0:T(8,128)S(1)}, f32[128,2048]{1,0:T(8,128)S(1)}, u32[]{:S(2)}, u32[]{:S(2)}) collective-permute-start(f32[128,2048]{1,0:T(8,128)S(1)} %add.101), channel_id=1, source_target_pairs={{0,2},{1,3},{2,0},{3,1},{4,6},{5,7},{6,4},{7,5},{8,10},{9,11},{10,... | collective-permute-start | bytes 3145736 | tf_op jit(solution)/shard_map/ppermute | solution.py:102
  135.6 51.6 %copy-start.5 = (f32[2048]{0:T(1024)S(1)}, f32[2048]{0:T(1024)}, u32[]{:S(2)}) copy-start(f32[2048]{0:T(1024)} %param.30) | copy-start | bytes 24580
  135.6 25.1 %collective-permute-start.2 = (f32[128,2048]{1,0:T(8,128)S(1)}, f32[128,2048]{1,0:T(8,128)S(1)}, u32[]{:S(2)}, u32[]{:S(2)}) collective-permute-start(f32[128,2048]{1,0:T(8,128)S(1)} %add.102), channel_id=1, source_target_pairs={{0,4},{1,5},{2,6},{3,7},{4,0},{5,1},{6,2},{7,3},{8,12},{9,13},{10,... | collective-permute-start | bytes 3145736 | tf_op jit(solution)/shard_map/ppermute | solution.py:102
  160.8 26.0 %collective-permute-start.3 = (f32[128,2048]{1,0:T(8,128)S(1)}, f32[128,2048]{1,0:T(8,128)S(1)}, u32[]{:S(2)}, u32[]{:S(2)}) collective-permute-start(f32[128,2048]{1,0:T(8,128)S(1)} %add.103), channel_id=1, source_target_pairs={{0,8},{1,9},{2,10},{3,11},{4,12},{5,13},{6,14},{7,15},{8,0},{9,1},... | collective-permute-start | bytes 3145736 | tf_op jit(solution)/shard_map/ppermute | solution.py:102
  187.2 14.4 %copy-start.2 = (s32[128]{0:T(128)S(1)}, s32[128]{0:T(128)}, u32[]{:S(2)}) copy-start(s32[128]{0:T(128)} %param.22) | copy-start | bytes 1540
  187.2 15.6 %copy-start.1 = (f32[128]{0:T(128)S(1)}, f32[128]{0:T(128)}, u32[]{:S(2)}) copy-start(f32[128]{0:T(128)} %param.23) | copy-start | bytes 1540
  201.5 3.8 %collective-permute-start.4 = (bf16[128,6400]{1,0:T(8,128)(2,1)}, bf16[128,6400]{1,0:T(8,128)(2,1)}, u32[]{:S(2)}, u32[]{:S(2)}) collective-permute-start(bf16[128,6400]{1,0:T(8,128)(2,1)} %get-tuple-element.14), channel_id=1, source_target_pairs={{0,16},{16,0},{1,17},{17,1},{2,18},{18,2},{3,19},{19,3},{4,20},{20... | collective-permute-start | bytes 4915208 | tf_op jit(solution)/shard_map/ppermute | solution.py:13
